TPU v7x, 32 devices: a whole 2x2x4 slice. The times are simulated.
32 devices in a mesh: conv: 2 (over x), seq: 8 (over z, y), head: 2 (over core).
Axes of the slice: x: 2, y: 2, z: 4, core: 2. Of those that a mesh axis runs over, the one named last changes fastest.
Arguments:
- queries: bfloat16 [3072, 2048], P(('conv', 'seq'), 'head'), parts along dimension 0, may hold values from -10 to 10, as said below
- key_states: bfloat16 [3072, 512], P(('conv', 'seq'), 'head'), parts along dimension 0, may hold values from -5 to 5, as said below
- value_states: bfloat16 [3072, 512], P(('conv', 'seq'), 'head'), parts along dimension 0, may hold values from -16 to 16
- out_weight: bfloat16 [2048, 4096], P('head'), may hold values from -0.125 to 0.125
- turn_lengths: int32 [32], P('conv'), parts along dimension 0, may hold values from 1 to 959, as said below
- block_flags: int32 [16, 8], P(('conv', 'seq')), parts along dimension 0, may hold values 0 or 1
Outputs:
- pooled: float32 [32, 4096], P(('conv', 'seq'), 'head'), parts along dimension 0
There are 2 independent parts, one for each index of `conv`. A program takes and returns all parts, laid end to end along the dimension named above; an argument that names none is the same for every part. Nothing has to cross between parts.
Inputs may be any that keep to these rules, and one draw needn't show every extreme that they name: `queries`: every entry lies within the stated bounds. `key_states`: every entry lies within the stated bounds. `turn_lengths`: the lengths sum to 1536; turn 0 has one token and turn 1, the longest, has exactly 959 tokens.
All inputs are finite; a program needn't handle non-finite values. No bound on the sum of `block_flags` on one device may be relied on, other than what follows from the above.
Results may differ from a plain program's by a relative error of at most 0.0035.
Values may be sent and summed in bfloat16 or wider, within the bound.
A program may use at most 128 MiB of HBM per device.

v0:
```python
import math
import jax
import jax.numpy as jnp
from jax import lax
from jax.sharding import PartitionSpec as P

HD = 128
big_negative = -1e30
log_two_e = 1.4426950408889634


def on_device(queries, key_states, value_states, out_weight, turn_lengths, block_flags):
    q_rows = queries.shape[0]
    heads_here = queries.shape[1] // HD
    groups = key_states.shape[1] // HD
    repeat = heads_here // groups
    factor = log_two_e / math.sqrt(HD)
    my_index = lax.axis_index("seq")
    own_pos = my_index * q_rows + jnp.arange(q_rows, dtype=jnp.int32)
    block_count = block_flags.shape[1]
    row_pick = jnp.zeros((q_rows,), jnp.int32)
    query_block = own_pos // q_rows
    grouped = queries.reshape(q_rows, groups, repeat, HD)

    def mask_for(key_start, length):
        key_pos = key_start + jnp.arange(length, dtype=jnp.int32)
        key_block = key_pos // q_rows
        hits = key_block[:, None] == jnp.arange(block_count, dtype=jnp.int32)[None, :]
        allowed = jnp.sum(jnp.where(hits[None], block_flags[:, None, :], 0), axis=2)
        allowed_rows = jnp.where(row_pick[:, None] == 1, allowed[-1][None, :], allowed[0][None, :])
        causal = key_pos[None, :] <= own_pos[:, None]
        return causal & ((key_block[None, :] == query_block[:, None]) | (allowed_rows == 1))

    def attend(state, key_rows, value_rows, key_start):
        run_top, run_sum, totals = state
        length = key_rows.shape[0]
        visible = mask_for(key_start, length)[None, None]
        logit = (
            jnp.einsum(
                "qgrd,kgd->grqk",
                grouped,
                key_rows.reshape(length, groups, HD),
                preferred_element_type=jnp.float32,
            )
            * factor
        )
        logit = jnp.where(visible, logit, big_negative)
        new_top = jnp.maximum(run_top, jnp.ceil(jnp.max(logit, axis=-1)))
        weights = jnp.where(visible, jnp.exp2(logit - new_top[..., None]), 0.0)
        rescale = jnp.exp2(run_top - new_top)
        run_sum = run_sum * rescale + jnp.sum(weights, axis=-1)
        update = jnp.einsum(
            "grqk,kgd->grqd",
            weights.astype(jnp.bfloat16),
            value_rows.reshape(length, groups, HD),
            preferred_element_type=jnp.float32,
        )
        totals = totals * rescale[..., None] + update
        return (new_top, run_sum, totals)

    start_state = (
        jnp.full((groups, repeat, q_rows), big_negative, jnp.float32),
        jnp.zeros((groups, repeat, q_rows), jnp.float32),
        jnp.zeros((groups, repeat, q_rows, HD), jnp.float32),
    )
    key_piece = lax.all_gather(key_states, "seq", axis=0, tiled=True)
    value_piece = lax.all_gather(value_states, "seq", axis=0, tiled=True)
    length = key_piece.shape[0]
    width_step = math.gcd(length, 1024)

    def one_block(number, carried):
        offset = number * width_step
        key_rows = lax.dynamic_slice_in_dim(key_piece, offset, width_step, 0)
        value_rows = lax.dynamic_slice_in_dim(value_piece, offset, width_step, 0)
        return attend(carried, key_rows, value_rows, offset)

    run_top, run_sum, totals = lax.fori_loop(0, length // width_step, one_block, start_state)
    attended_work = (
        (totals / run_sum[..., None])
        .transpose(2, 0, 1, 3)
        .reshape(q_rows, heads_here * HD)
        .astype(jnp.bfloat16)
    )
    turn_ends = jnp.cumsum(turn_lengths)
    starts = turn_ends - turn_lengths
    member = (starts[:, None] <= own_pos[None, :]) & (own_pos[None, :] < turn_ends[:, None])
    turn_share = jnp.where(member, 1.0, 0.0).astype(jnp.float32) / turn_lengths[:, None].astype(
        jnp.float32
    )
    partial_rows = jnp.dot(attended_work, out_weight, preferred_element_type=jnp.float32)
    projected_rows = lax.psum_scatter(partial_rows, "head", scatter_dimension=1, tiled=True)
    pooled_part = jnp.dot(turn_share, projected_rows, precision=lax.Precision.HIGHEST)
    return lax.psum_scatter(pooled_part, "seq", scatter_dimension=0, tiled=True)


def solution(mesh):
    in_specs = (
        P(("conv", "seq"), "head"),
        P(("conv", "seq"), "head"),
        P(("conv", "seq"), "head"),
        P("head", None),
        P("conv"),
        P(("conv", "seq"), None),
    )
    out_specs = P(("conv", "seq"), "head")
    return jax.shard_map(
        on_device, mesh=mesh, in_specs=in_specs, out_specs=out_specs, check_vma=False
    )
```

profile of v0, /device:TPU:0, one launch (start us, length us, event | category | flops | bytes accessed | tf_op | source)
XLA Modules:
  0.0 211.3 jit_solution(6904133844643909026)
XLA Ops:
  6.5 0.0 copy-start
  6.5 0.0 reduce-scatter.2.cloned.1.call-start
  6.5 36.3 %all_gather.6 = bf16[1536,256]{1,0:T(8,128)(2,1)} all-gather(bf16[192,256]{1,0:T(8,128)(2,1)} %param.9), channel_id=1, replica_groups=mesh['conv'=2,'seq'=8,'head'=2] {'seq'}, dimensions={0}, use_global_device_ids=true | all-gather | bytes 884736 | tf_op jit(solution)/shard_map/all_gather | solution.py:66
  42.9 34.2 %all_gather.7 = bf16[1536,256]{1,0:T(8,128)(2,1)} all-gather(bf16[192,256]{1,0:T(8,128)(2,1)} %param.10), channel_id=1, replica_groups=mesh['conv'=2,'seq'=8,'head'=2] {'seq'}, dimensions={0}, use_global_device_ids=true | all-gather | bytes 884736 | tf_op jit(solution)/shard_map/all_gather | solution.py:67
  77.1 1.3 reshape.229
  78.4 0.8 copy.26
  79.2 0.0 copy-done
  79.2 28.0 %while.22 = (s32[]{:T(128)}, f32[2,4,192]{2,1,0:T(4,128)S(1)}, f32[2,4,192]{2,1,0:T(4,128)S(1)}, f32[2,4,192,128]{3,2,1,0:T(8,128)}, s32[1,8]{1,0:T(1,128)S(1)},...) while((s32[]{:T(128)}, f32[2,4,192]{2,1,0:T(4,128)S(1)}, ...), condition=%wide.region_5.6_spmd.clone.clone.clone, body=%wide.region_1.5_spmd.clone.clone.clone.sunk | while | flops 415462080 | bytes 14534883 | solution.py:77
  79.2 0.1 select_reduce_fusion.2
  79.3 0.2 or_and_fusion.2
  79.5 1.1 constant_dynamic-slice_fusion.4
  80.6 0.8 copy.39
  81.4 1.8 fusion.54
  83.3 1.2 fusion.55
  84.5 0.8 copy.40
  85.3 3.1 %fusion.57 = f32[2,4,192,128]{3,2,1,0:T(8,128)} fusion(bf16[512,2,128,1]{0,2,3,1:T(8,128)(2,1)} %bitcast.53, f32[2,512,192,4]{1,2,3,0:T(8,128)S(1)} %get-tuple-element.465, f32[2,4,192]{2,1,0:T(4,128)S(1)} %ceil_maximum_fusion.2, pred[192,512]{1,0:T(8,128)(4,1)S(1)} %or_and_fusion.2, f32[2,4,192,128]{3,2,1,0:T(8,128)} %get-tuple-element.485, ...), kind=kOutput, calls=%fused_computation.9.clone.1 | convolution fusion | flops 206635008 | bytes 5091329 | tf_op jit(solution)/shard_map/while/body/eval_jaxpr/grqk,kgd->grqd/dot_general | solution.py:52
  88.5 0.1 select_reduce_fusion.2
  88.6 0.2 or_and_fusion.2
  88.8 1.1 constant_dynamic-slice_fusion.4
  89.8 0.8 copy.39
  90.7 1.8 fusion.54
  92.5 1.2 fusion.55
  93.8 0.8 copy.40
  94.6 3.2 %fusion.57 = f32[2,4,192,128]{3,2,1,0:T(8,128)} fusion(bf16[512,2,128,1]{0,2,3,1:T(8,128)(2,1)} %bitcast.53, f32[2,512,192,4]{1,2,3,0:T(8,128)S(1)} %get-tuple-element.465, f32[2,4,192]{2,1,0:T(4,128)S(1)} %ceil_maximum_fusion.2, pred[192,512]{1,0:T(8,128)(4,1)S(1)} %or_and_fusion.2, f32[2,4,192,128]{3,2,1,0:T(8,128)} %get-tuple-element.485, ...), kind=kOutput, calls=%fused_computation.9.clone.1 | convolution fusion | flops 206635008 | bytes 5091329 | tf_op jit(solution)/shard_map/while/body/eval_jaxpr/grqk,kgd->grqd/dot_general | solution.py:52
  97.8 0.1 select_reduce_fusion.2
  98.0 0.2 or_and_fusion.2
  98.1 1.1 constant_dynamic-slice_fusion.4
  99.2 0.8 copy.39
  100.1 1.8 fusion.54
  101.9 1.2 fusion.55
  103.1 0.8 copy.40
  104.0 3.2 %fusion.57 = f32[2,4,192,128]{3,2,1,0:T(8,128)} fusion(bf16[512,2,128,1]{0,2,3,1:T(8,128)(2,1)} %bitcast.53, f32[2,512,192,4]{1,2,3,0:T(8,128)S(1)} %get-tuple-element.465, f32[2,4,192]{2,1,0:T(4,128)S(1)} %ceil_maximum_fusion.2, pred[192,512]{1,0:T(8,128)(4,1)S(1)} %or_and_fusion.2, f32[2,4,192,128]{3,2,1,0:T(8,128)} %get-tuple-element.485, ...), kind=kOutput, calls=%fused_computation.9.clone.1 | convolution fusion | flops 206635008 | bytes 5091329 | tf_op jit(solution)/shard_map/while/body/eval_jaxpr/grqk,kgd->grqd/dot_general | solution.py:52
  107.2 1.4 fusion.19
  108.6 0.3 copy.28
  108.9 0.3 convert_element_type.26
  109.2 6.9 %fusion.35 = f32[192,4096]{1,0:T(8,128)} fusion(bf16[192,1024]{1,0:T(8,128)(2,1)S(1)} %convert_element_type.26, bf16[1024,4096]{1,0:T(8,128)(2,1)} %param.11), kind=kOutput, calls=%fused_computation.51 | convolution fusion | flops 1610612736 | bytes 11927552 | tf_op jit(solution)/shard_map/dot_general | solution.py:90
  116.1 0.0 copy-start.1
  116.1 0.0 copy-start.2
  116.1 0.0 reduce-scatter.2.cloned.1.call-update
  116.1 0.0 all-reduce.3.cloned.1.call-start
  116.1 0.6 copy-done.1
  116.7 0.1 copy.24
  116.8 0.1 reduce.6
  117.0 11.5 %reduce-scatter.2.cloned.1.call-done = f32[192,2048]{1,0:T(8,128)} async-done(((f32[192,4096]{1,0:T(8,128)}), f32[192,2048]{1,0:T(8,128)}) %reduce-scatter.2.cloned.1.call-update) | async-done | bytes 1572880 | tf_op jit(solution)/shard_map/reduce_scatter | solution.py:91
  128.5 2.9 %fusion.20 = f32[16,2048]{1,0:T(8,128)} fusion(f32[192,2048]{1,0:T(8,128)} %reduce-scatter.2.cloned.1.call-done, f32[16]{0:T(128)S(1)} %get-tuple-element.393, s32[192]{0:T(256)S(1)} %iota_add_fusion.2, s32[16]{0:T(128)S(1)} %reduce.6, s32[16]{0:T(128)S(1)} %get-tuple-element.392), kind=kOutput, calls=%fused_computation.34 | convolution fusion | flops 75512832 | bytes 1704896 | tf_op jit(solution)/shard_map/dot_general | solution.py:92
  131.4 0.0 all-reduce.3.cloned.1.call-update
  131.4 0.0 copy-done.2
  131.4 0.6 dynamic-slice
  132.6 70.4 %all-reduce.3.cloned.1.call-done = f32[16,2048]{1,0:T(8,128)} async-done(((f32[16,2048]{1,0:T(8,128)}), f32[16,2048]{1,0:T(8,128)}) %all-reduce.3.cloned.1.call-update) | async-done | bytes 131088
  203.0 1.5 constant_dynamic-slice_fusion.2
  (24 shorter events, 0.2 us)
Async XLA Ops:
  6.5 72.6 %copy-start = (s32[1,8]{1,0:T(1,128)S(1)}, s32[1,8]{1,0:T(1,128)}, u32[]{:S(2)}) copy-start(s32[1,8]{1,0:T(1,128)} %param.13) | copy-start | bytes 100
  6.5 121.9 %reduce-scatter.2.cloned.1.call-start = ((), (), s32[]{:S(2)}) async-start(), calls=%async_computation.1 | async-start | bytes 4718592 | tf_op jit(solution)/shard_map/reduce_scatter | solution.py:91
  116.1 0.7 copy-start.1
  116.1 15.3 %copy-start.2 = (u32[32]{0:T(128)S(1)}, u32[32]{0:T(128)}, u32[]{:S(2)}) copy-start(u32[32]{0:T(128)} %constant.141) | copy-start | bytes 388
  116.1 86.9 %all-reduce.3.cloned.1.call-start = ((), (), s32[]{:S(2)}) async-start(), calls=%async_computation.2 | async-start | bytes 262144
Sparse Core Ops, SparseCore 0:
  116.2 12.2 reduce-scatter.1
  132.2 70.7 all-reduce.2
where the time goes:
time: 212 us; the launch traced here: 211 us
  waiting for transfers between devices  81.9 us (39%)
  blocking collectives  70.6 us (33%)
  matrix products  24.8 us (12%)
  between operations  14.1 us (7%)
  local copies, waits for them, and re-layouts  13.6 us (6%)
  other arithmetic  6.13 us (3%)
    unnamed x3, waiting for transfers between devices  70.4 us
    all_gather x1, blocking collectives, on_device(): key_piece = lax.all_gather(key_states, 'seq', axis=0, tiled=True)  36.3 us
    all_gather x1, blocking collectives, on_device(): value_piece = lax.all_gather(value_states, 'seq', axis=0, tiled=True)  34.2 us
    reduce_scatter x1, waiting for transfers between devices, on_device(): lax.psum_scatter(partial_rows, 'head', scatter_dimension=1, tiled=True)  11.5 us
    dot_general x3, matrix products, attend(): jnp.einsum('grqk,kgd->grqd', weights.astype(jnp.bfloat16), value_rows.res...  9.53 us
    dot_general x1, matrix products, on_device(): jnp.dot(attended_work, out_weight, preferred_element_type=jnp.float32)  6.85 us
    dynamic_slice x6, local copies, waits for them, and re-layouts, one_block(): value_rows = lax.dynamic_slice_in_dim(value_piece, offset, width_step, 0)  5.76 us
    dot_general x3, matrix products, attend(): jnp.einsum('qgrd,kgd->grqk', grouped, key_rows.reshape(length, groups, HD...  5.5 us
  transfers between devices with their start and end apart: 2, of which 2 were waited for; matrix products, arithmetic and copies ran while one was open for 0% of the time, Pallas kernels for 0%

commit v1 on v0

--- a/solution.py
+++ b/solution.py
@@ -3,6 +3,7 @@
 import jax.numpy as jnp
 from jax import lax
 from jax.sharding import PartitionSpec as P
+from jax.lax import all_gather
 
 HD = 128
 big_negative = -1e30
@@ -63,8 +64,12 @@
         jnp.zeros((groups, repeat, q_rows), jnp.float32),
         jnp.zeros((groups, repeat, q_rows, HD), jnp.float32),
     )
-    key_piece = lax.all_gather(key_states, "seq", axis=0, tiled=True)
-    value_piece = lax.all_gather(value_states, "seq", axis=0, tiled=True)
+    proceed_tasks = lambda patch, u: jnp.split(
+        all_gather(jnp.concatenate([u, patch], 1), axis_name="seq", axis=0, tiled=True),
+        [u.shape[1]],
+        1,
+    )
+    key_piece, value_piece = proceed_tasks(value_states, key_states)
     length = key_piece.shape[0]
     width_step = math.gcd(length, 1024)
 

time: 212 us -> 189 us (0.89)
  blocking collectives: 70.6 us -> 0 us
  waiting for transfers between devices: 81.9 us -> 125 us
  local copies, waits for them, and re-layouts: 13.6 us -> 16.2 us
    all_gather x2 -> x0, blocking collectives: 70.6 us -> none  [the longest x1 36.3 us: on_device(): key_piece = lax.all_gather(key_states, 'seq', axis=0, tiled=True)]
    all_gather x0 -> x1, waiting for transfers between devices: none -> 46.1 us  [on_device(): all_gather(jnp.concatenate([u, patch], 1), axis_name='seq', axis=0, tiled...]
    split x0 -> x1, local copies, waits for them, and re-layouts: none -> 2.62 us  [on_device(): jnp.split(all_gather(jnp.concatenate([u, patch], 1), axis_name='seq', axi...]
    reduce_scatter x1, waiting for transfers between devices: 11.5 us -> 8.99 us  [on_device(): lax.psum_scatter(partial_rows, 'head', scatter_dimension=1, tiled=True)]
    unnamed x3 -> x4, waiting for transfers between devices: 70.4 us -> 70.4 us
  transfers between devices with their start and end apart: 2 -> 3, of which waited for: 2 -> 3; matrix products, arithmetic and copies ran while one was open for 0% -> 2% of each run, Pallas kernels for 0% -> 0%
where the time goes in v1:
time: 189 us; the launch traced here: 188 us
  waiting for transfers between devices  125 us (66%)
  matrix products  24.8 us (13%)
  local copies, waits for them, and re-layouts  16.2 us (9%)
  between operations  13.8 us (7%)
  other arithmetic  7.76 us (4%)
    unnamed x4, waiting for transfers between devices  70.4 us
    all_gather x1, waiting for transfers between devices, on_device(): all_gather(jnp.concatenate([u, patch], 1), axis_name='seq', axis=0, tiled...  46.1 us
    dot_general x3, matrix products, attend(): jnp.einsum('grqk,kgd->grqd', weights.astype(jnp.bfloat16), value_rows.res...  9.55 us
    reduce_scatter x1, waiting for transfers between devices, on_device(): lax.psum_scatter(partial_rows, 'head', scatter_dimension=1, tiled=True)  8.99 us
    dot_general x1, matrix products, on_device(): jnp.dot(attended_work, out_weight, preferred_element_type=jnp.float32)  6.85 us
    dynamic_slice x6, local copies, waits for them, and re-layouts, one_block(): value_rows = lax.dynamic_slice_in_dim(value_piece, offset, width_step, 0)  5.72 us
    dot_general x3, matrix products, attend(): jnp.einsum('qgrd,kgd->grqk', grouped, key_rows.reshape(length, groups, HD...  5.5 us
  transfers between devices with their start and end apart: 3, of which 3 were waited for; matrix products, arithmetic and copies ran while one was open for 2% of the time, Pallas kernels for 0%

profile of v1, /device:TPU:0, one launch (start us, length us, event | category | flops | bytes accessed | tf_op | source)
XLA Modules:
  0.0 188.3 jit_solution(15696550019272096463)
XLA Ops:
  6.5 0.0 copy-start
  6.5 0.0 all-gather.2.cloned.1.call-start
  6.5 1.6 pad_maximum_fusion
  8.2 0.0 all-gather.2.cloned.1.call-update
  8.2 0.0 reduce-scatter.2.cloned.1.call-start
  8.3 1.3 reshape.229
  9.5 0.8 copy.26
  10.3 46.1 %all-gather.2.cloned.1.call-done = bf16[1536,512]{1,0:T(8,128)(2,1)} async-done(((bf16[192,512]{1,0:T(8,128)(2,1)}), bf16[1536,512]{1,0:T(8,128)(2,1)}) %all-gather.2.cloned.1.call-update) | async-done | bytes 1572880 | tf_op jit(solution)/shard_map/all_gather | solution.py:68
  56.5 2.6 %fusion.34 = (bf16[1536,256]{1,0:T(8,128)(2,1)}, bf16[1536,256]{1,0:T(8,128)(2,1)}) fusion(bf16[1536,512]{1,0:T(8,128)(2,1)} %all-gather.2.cloned.1.call-done), kind=kLoop, calls=%fused_computation.51 | loop fusion | bytes 3145728 | tf_op jit(solution)/shard_map/split | solution.py:67
  59.1 0.0 copy-done
  59.1 28.0 %while.22 = (s32[]{:T(128)}, f32[2,4,192]{2,1,0:T(4,128)S(1)}, f32[2,4,192]{2,1,0:T(4,128)S(1)}, f32[2,4,192,128]{3,2,1,0:T(8,128)}, s32[1,8]{1,0:T(1,128)S(1)},...) while((s32[]{:T(128)}, f32[2,4,192]{2,1,0:T(4,128)S(1)}, ...), condition=%wide.region_5.6_spmd.clone.clone.clone, body=%wide.region_1.5_spmd.clone.clone.clone.sunk | while | flops 415462080 | bytes 14534883 | solution.py:82
  59.1 0.1 select_reduce_fusion.2
  59.2 0.2 or_and_fusion.2
  59.4 1.1 constant_dynamic-slice_fusion.4
  60.5 0.8 copy.39
  61.3 1.8 fusion.55
  63.2 1.2 fusion.56
  64.4 0.8 copy.40
  65.2 3.1 %fusion.58 = f32[2,4,192,128]{3,2,1,0:T(8,128)} fusion(bf16[512,2,128,1]{0,2,3,1:T(8,128)(2,1)} %bitcast.53, f32[2,512,192,4]{1,2,3,0:T(8,128)S(1)} %get-tuple-element.467, f32[2,4,192]{2,1,0:T(4,128)S(1)} %ceil_maximum_fusion.2, pred[192,512]{1,0:T(8,128)(4,1)S(1)} %or_and_fusion.2, f32[2,4,192,128]{3,2,1,0:T(8,128)} %get-tuple-element.487, ...), kind=kOutput, calls=%fused_computation.9.clone.1 | convolution fusion | flops 206635008 | bytes 5091329 | tf_op jit(solution)/shard_map/while/body/eval_jaxpr/grqk,kgd->grqd/dot_general | solution.py:53
  68.3 0.1 select_reduce_fusion.2
  68.4 0.2 or_and_fusion.2
  68.6 1.1 constant_dynamic-slice_fusion.4
  69.7 0.8 copy.39
  70.5 1.8 fusion.55
  72.4 1.2 fusion.56
  73.6 0.8 copy.40
  74.5 3.2 %fusion.58 = f32[2,4,192,128]{3,2,1,0:T(8,128)} fusion(bf16[512,2,128,1]{0,2,3,1:T(8,128)(2,1)} %bitcast.53, f32[2,512,192,4]{1,2,3,0:T(8,128)S(1)} %get-tuple-element.467, f32[2,4,192]{2,1,0:T(4,128)S(1)} %ceil_maximum_fusion.2, pred[192,512]{1,0:T(8,128)(4,1)S(1)} %or_and_fusion.2, f32[2,4,192,128]{3,2,1,0:T(8,128)} %get-tuple-element.487, ...), kind=kOutput, calls=%fused_computation.9.clone.1 | convolution fusion | flops 206635008 | bytes 5091329 | tf_op jit(solution)/shard_map/while/body/eval_jaxpr/grqk,kgd->grqd/dot_general | solution.py:53
  77.7 0.1 select_reduce_fusion.2
  77.8 0.2 or_and_fusion.2
  78.0 1.1 constant_dynamic-slice_fusion.4
  79.1 0.8 copy.39
  79.9 1.8 fusion.55
  81.8 1.2 fusion.56
  83.0 0.8 copy.40
  83.8 3.2 %fusion.58 = f32[2,4,192,128]{3,2,1,0:T(8,128)} fusion(bf16[512,2,128,1]{0,2,3,1:T(8,128)(2,1)} %bitcast.53, f32[2,512,192,4]{1,2,3,0:T(8,128)S(1)} %get-tuple-element.467, f32[2,4,192]{2,1,0:T(4,128)S(1)} %ceil_maximum_fusion.2, pred[192,512]{1,0:T(8,128)(4,1)S(1)} %or_and_fusion.2, f32[2,4,192,128]{3,2,1,0:T(8,128)} %get-tuple-element.487, ...), kind=kOutput, calls=%fused_computation.9.clone.1 | convolution fusion | flops 206635008 | bytes 5091329 | tf_op jit(solution)/shard_map/while/body/eval_jaxpr/grqk,kgd->grqd/dot_general | solution.py:53
  87.1 1.4 fusion.19
  88.5 0.3 copy.28
  88.8 0.3 convert_element_type.26
  89.1 6.9 %fusion.36 = f32[192,4096]{1,0:T(8,128)} fusion(bf16[192,1024]{1,0:T(8,128)(2,1)S(1)} %convert_element_type.26, bf16[1024,4096]{1,0:T(8,128)(2,1)} %param.11), kind=kOutput, calls=%fused_computation.53 | convolution fusion | flops 1610612736 | bytes 11927552 | tf_op jit(solution)/shard_map/dot_general | solution.py:95
  95.9 0.0 copy-start.1
  95.9 0.0 copy-start.2
  95.9 0.0 reduce-scatter.2.cloned.1.call-update
  95.9 0.0 all-reduce.3.cloned.1.call-start
  96.0 0.6 copy-done.1
  96.6 0.1 copy.24
  96.7 0.1 reduce.6
  96.8 9.0 %reduce-scatter.2.cloned.1.call-done = f32[192,2048]{1,0:T(8,128)} async-done(((f32[192,4096]{1,0:T(8,128)}), f32[192,2048]{1,0:T(8,128)}) %reduce-scatter.2.cloned.1.call-update) | async-done | bytes 1572880 | tf_op jit(solution)/shard_map/reduce_scatter | solution.py:96
  105.8 2.9 %fusion.20 = f32[16,2048]{1,0:T(8,128)} fusion(f32[192,2048]{1,0:T(8,128)} %reduce-scatter.2.cloned.1.call-done, f32[16]{0:T(128)S(1)} %get-tuple-element.395, s32[192]{0:T(256)S(1)} %iota_add_fusion.2, s32[16]{0:T(128)S(1)} %reduce.6, s32[16]{0:T(128)S(1)} %get-tuple-element.394), kind=kOutput, calls=%fused_computation.35 | convolution fusion | flops 75512832 | bytes 1704896 | tf_op jit(solution)/shard_map/dot_general | solution.py:97
  108.7 0.0 all-reduce.3.cloned.1.call-update
  108.7 0.0 copy-done.2
  108.8 0.6 dynamic-slice
  110.0 70.3 %all-reduce.3.cloned.1.call-done = f32[16,2048]{1,0:T(8,128)} async-done(((f32[16,2048]{1,0:T(8,128)}), f32[16,2048]{1,0:T(8,128)}) %all-reduce.3.cloned.1.call-update) | async-done | bytes 131088
  180.3 1.5 constant_dynamic-slice_fusion.2
  (24 shorter events, 0.2 us)
Async XLA Ops:
  6.5 52.5 %copy-start = (s32[1,8]{1,0:T(1,128)S(1)}, s32[1,8]{1,0:T(1,128)}, u32[]{:S(2)}) copy-start(s32[1,8]{1,0:T(1,128)} %param.13) | copy-start | bytes 100
  6.5 49.9 %all-gather.2.cloned.1.call-start = ((), (), s32[]{:S(2)}) async-start(), calls=%async_computation.1 | async-start | bytes 1769472 | tf_op jit(solution)/shard_map/all_gather | solution.py:68
  8.2 97.6 %reduce-scatter.2.cloned.1.call-start = ((), (), s32[]{:S(2)}) async-start(), calls=%async_computation.2 | async-start | bytes 4718592 | tf_op jit(solution)/shard_map/reduce_scatter | solution.py:96
  95.9 0.7 copy-start.1
  95.9 12.8 %copy-start.2 = (u32[32]{0:T(128)S(1)}, u32[32]{0:T(128)}, u32[]{:S(2)}) copy-start(u32[32]{0:T(128)} %constant.141) | copy-start | bytes 388
  95.9 84.4 %all-reduce.3.cloned.1.call-start = ((), (), s32[]{:S(2)}) async-start(), calls=%async_computation.3 | async-start | bytes 262144
Sparse Core Ops, SparseCore 0:
  9.5 46.8 all-gather.1
  96.1 9.7 reduce-scatter.1
  109.5 70.7 all-reduce.2
